TPU v7x, 256 devices: a whole 4x4x8 slice. The times are simulated.
256 devices in a mesh: row: 16 (over z, core), col: 16 (over x, y).
Axes of the slice: x: 4, y: 4, z: 8, core: 2. Of those that a mesh axis runs over, the one named last changes fastest.
Arguments:
- tiles: float32 [16, 16, 16, 128, 128], P('row', 'col'), may hold values from -1 to 1
- tile_rows: int32 [16, 16, 16], P('row', 'col'), may hold values from 0 to 63, as said below
- tile_cols: int32 [16, 16, 16], P('row', 'col'), may hold values from 0 to 63
- tile_counts: int32 [16, 16], P('row', 'col'), may hold values from 2 to 16, as said below
- objective: float32 [131072], P('col'), may hold values from -6 to 6
- upper: float32 [131072], P('col'), may hold values from 0.2 to 2
- bound_codes: int32 [131072], P('col'), may hold values from 0 to 2
- rhs: float32 [131072], P('row'), may hold values from -6 to 6
- row_codes: int32 [131072], P('row'), may hold values from 0 to 1
Outputs:
- primal: float32 [131072], P('col')
- dual: float32 [131072], P('row')
Inputs may be any that keep to these rules, and one draw needn't show every extreme that they name: `tile_rows`: one device's live slots hold distinct (tile row, tile column) pairs. `tile_counts`: slots at or past a device's count are not part of K; some device has all 16 slots live.
All inputs are finite; a program needn't handle non-finite values. Where the computation divides by a largest or mean magnitude, that divisor is 1e-20 or more.
Results may differ from a plain program's by a relative error of at most 0.00018.
Values sent between devices are 32-bit elements; how exact they have to be, the bound alone decides.
A program may use at most 64 MiB of HBM per device.

v0:
```python
import jax
import jax.numpy as jnp
from jax import lax
from jax.sharding import PartitionSpec as P

TILE_BLOCK = 16
TILE_ROWS = 64
TILE_COLS = 64
OUTER = 2
INNER = 4


def project_primal(values, bound_codes, upper):
    values = jnp.where(bound_codes >= 1, jnp.maximum(values, 0.0), values)
    return jnp.where(bound_codes == 2, jnp.minimum(values, upper), values)


def project_dual(values, row_codes):
    return jnp.where(row_codes == 1, jnp.maximum(values, 0.0), values)


def step_update(step_size, weight, inter_term, primal_sq, dual_sq, counter):
    shrink = 1.0 - (counter + 1) ** (-0.3)
    growth = 1.0 + (counter + 1) ** (-0.6)
    numer = shrink * (weight * primal_sq + dual_sq / weight + 1e-06)
    return numer / jnp.maximum(2.0 * jnp.abs(inter_term), numer / (growth * step_size))


def tile_products(tile_data, row_slots, col_slots, live_count, vector, direction):
    highest = lax.Precision.HIGHEST
    width = tile_data.shape[-1]
    groups = (live_count + TILE_BLOCK - 1) // TILE_BLOCK
    if direction == "forward":
        shaped = vector.reshape(TILE_COLS, width)
        out_rows = TILE_ROWS
    else:
        shaped = vector.reshape(TILE_ROWS, width)
        out_rows = TILE_COLS

    def visit(group, total):
        first_slot = group * TILE_BLOCK
        alive = (first_slot + jnp.arange(TILE_BLOCK, dtype=jnp.int32) < live_count).astype(
            jnp.float32
        )
        row_hot = (row_slots[:, None] == jnp.arange(TILE_ROWS, dtype=jnp.int32)[None, :]).astype(
            jnp.float32
        )
        col_hot = (col_slots[:, None] == jnp.arange(TILE_COLS, dtype=jnp.int32)[None, :]).astype(
            jnp.float32
        )
        if direction == "forward":
            pieces = jnp.dot(col_hot, shaped, precision=highest)
            images = jnp.einsum("tij,tj->ti", tile_data, pieces, precision=highest)
            return total + jnp.einsum(
                "tk,ti->ki", row_hot * alive[:, None], images, precision=highest
            )
        else:
            pieces = jnp.dot(row_hot, shaped, precision=highest)
            images = jnp.einsum("tij,ti->tj", tile_data, pieces, precision=highest)
            return total + jnp.einsum(
                "tk,tj->kj", col_hot * alive[:, None], images, precision=highest
            )

    total = lax.fori_loop(0, groups, visit, jnp.zeros((out_rows, width), jnp.float32))
    return total.reshape(-1)


def per_device(
    tiles, tile_rows, tile_cols, tile_counts, objective, upper, bound_codes, rhs, row_codes
):
    tile_data = tiles[0, 0]
    row_slots = tile_rows[0, 0]
    col_slots = tile_cols[0, 0]
    live_count = tile_counts[0, 0]
    row_place = lax.axis_index("row")
    col_place = lax.axis_index("col")
    primal_mask = (row_place == 0).astype(jnp.float32)
    dual_mask = (col_place == 0).astype(jnp.float32)

    def forward(vector):
        partial_rows = tile_products(tile_data, row_slots, col_slots, live_count, vector, "forward")
        return lax.psum(partial_rows, "col")

    def backward(vector):
        partial_cols = tile_products(
            tile_data, row_slots, col_slots, live_count, vector, "backward"
        )
        return lax.psum(partial_cols, "row")

    def pair_sums(primal_term, dual_term):
        return lax.psum((primal_term * primal_mask, dual_term * dual_mask), ("row", "col"))

    alive_slots = (jnp.arange(tile_data.shape[0], dtype=jnp.int32) < live_count).astype(jnp.float32)
    local_largest = jnp.max(jnp.abs(tile_data) * alive_slots[:, None, None])
    largest = lax.pmax(local_largest, ("row", "col"))
    step_size = 0.05 / (largest + 1e-06)
    object_sq, rhs_sq = pair_sums(jnp.sum(objective * objective), jnp.sum(rhs * rhs))
    weight = jnp.sqrt((object_sq + 1e-06) / (rhs_sq + 1e-06))
    primal = jnp.zeros_like(objective)
    dual_piece = jnp.zeros_like(rhs)
    row_image = jnp.zeros_like(rhs)
    col_image = jnp.zeros_like(objective)
    counter = 0
    for cycle_index in range(OUTER):
        start_primal = primal
        start_dual = dual_piece
        primal_total = jnp.zeros_like(objective)
        dual_total = jnp.zeros_like(rhs)
        weight_total = jnp.zeros((), jnp.float32)
        for step_index in range(INNER):
            counter += 1
            next_primal = project_primal(
                primal - step_size / weight * (objective - col_image), bound_codes, upper
            )
            next_row = forward(next_primal)
            next_dual = project_dual(
                dual_piece + step_size * weight * (rhs - (2.0 * next_row - row_image)), row_codes
            )
            next_col = backward(next_dual)
            primal_move = next_primal - primal
            dual_move = next_dual - dual_piece
            inter_term, primal_sq, dual_sq = lax.psum(
                (
                    jnp.sum(primal_move * (next_col - col_image)) * primal_mask,
                    jnp.sum(primal_move * primal_move) * primal_mask,
                    jnp.sum(dual_move * dual_move) * dual_mask,
                ),
                ("row", "col"),
            )
            primal_total = primal_total + step_size * next_primal
            dual_total = dual_total + step_size * next_dual
            weight_total = weight_total + step_size
            step_size = step_update(step_size, weight, inter_term, primal_sq, dual_sq, counter)
            primal, dual_piece, row_image, col_image = (next_primal, next_dual, next_row, next_col)
        primal = primal_total / weight_total
        dual_piece = dual_total / weight_total
        primal_shift = primal - start_primal
        dual_shift = dual_piece - start_dual
        primal_drift, dual_drift = pair_sums(
            jnp.sum(primal_shift * primal_shift), jnp.sum(dual_shift * dual_shift)
        )
        weight = jnp.sqrt(weight * jnp.sqrt(dual_drift + 1e-06) / jnp.sqrt(primal_drift + 1e-06))
        if cycle_index + 1 < OUTER:
            row_image = forward(primal)
            col_image = backward(dual_piece)
    return (primal, dual_piece)


def solution(mesh):
    placed = (
        P("row", "col", None, None, None),
        P("row", "col", None),
        P("row", "col", None),
        P("row", "col"),
        P("col"),
        P("col"),
        P("col"),
        P("row"),
        P("row"),
    )
    return jax.shard_map(
        per_device, mesh=mesh, in_specs=placed, out_specs=(P("col"), P("row")), check_vma=False
    )
```

profile of v0, /device:TPU:1, one launch (start us, length us, event | category | flops | bytes accessed | tf_op | source)
XLA Modules:
  0.0 1711.0 jit_solution(5136370811758483441)
XLA Ops:
  10.5 81.4 %all-reduce.7 = (f32[]{:T(128)}, f32[]{:T(128)}) all-reduce(f32[]{:T(128)S(6)} %mul.700, f32[]{:T(128)S(6)} %mul.702), channel_id=1, replica_groups=mesh['row'=16,'col'=16] {'row','col'}, use_global_device_ids=true, to_apply=%region_1.0 | all-reduce | flops 2 | bytes 16 | tf_op jit(solution)/shard_map/psum | solution.py:91
  93.3 2.2 fusion.120
  95.5 72.7 %pmax.7 = f32[]{:T(128)} all-reduce(f32[]{:T(128)} %fusion.120), channel_id=1, replica_groups=mesh['row'=16,'col'=16] {'row','col'}, use_global_device_ids=true, to_apply=%region_5.0 | all-reduce | flops 1 | bytes 8 | tf_op jit(solution)/shard_map/pmax | solution.py:95
  169.8 1.7 fusion.117
  172.2 1.0 while.204
  173.2 56.8 %psum.297 = f32[8192]{0:T(1024)S(1)} all-reduce(f32[8192]{0:T(1024)S(1)} %bitcast.318), channel_id=1, replica_groups=mesh['row'=16,'col'=16] {'col'}, use_global_device_ids=true, to_apply=%region_10.11 | all-reduce | flops 8192 | bytes 65536 | tf_op jit(solution)/shard_map/psum | solution.py:82
  230.8 1.0 fusion.115
  231.8 1.0 while.205
  232.8 56.9 %psum.299 = f32[8192]{0:T(1024)S(1)} all-reduce(f32[8192]{0:T(1024)S(1)} %bitcast.319), channel_id=1, replica_groups=mesh['row'=16,'col'=16] {'row'}, use_global_device_ids=true, to_apply=%region_15.16 | all-reduce | flops 8192 | bytes 65536 | tf_op jit(solution)/shard_map/psum | solution.py:88
  292.4 74.0 %all-reduce.6 = (f32[]{:T(128)}, f32[]{:T(128)}, f32[]{:T(128)}) all-reduce(f32[]{:T(128)S(6)} %mul.708, f32[]{:T(128)S(6)} %mul.715, f32[]{:T(128)S(6)} %mul.717), channel_id=1, replica_groups=mesh['row'=16,'col'=16] {'row','col'}, use_global_device_ids=true, to_apply=%region_7.8 | all-reduce | flops 3 | bytes 24 | tf_op jit(solution)/shard_map/psum | solution.py:122
  368.6 1.7 fusion.113
  370.4 1.0 while.206
  371.4 57.7 %psum.302 = f32[8192]{0:T(1024)S(1)} all-reduce(f32[8192]{0:T(1024)S(1)} %bitcast.320), channel_id=1, replica_groups=mesh['row'=16,'col'=16] {'col'}, use_global_device_ids=true, to_apply=%region_22.23 | all-reduce | flops 8192 | bytes 65536 | tf_op jit(solution)/shard_map/psum | solution.py:82
  429.9 1.0 fusion.111
  430.9 1.0 while.207
  431.8 56.1 %psum.304 = f32[8192]{0:T(1024)S(1)} all-reduce(f32[8192]{0:T(1024)S(1)} %bitcast.321), channel_id=1, replica_groups=mesh['row'=16,'col'=16] {'row'}, use_global_device_ids=true, to_apply=%region_27.28 | all-reduce | flops 8192 | bytes 65536 | tf_op jit(solution)/shard_map/psum | solution.py:88
  487.9 0.7 multiply_reduce_fusion.17
  490.6 74.0 %all-reduce.5 = (f32[]{:T(128)}, f32[]{:T(128)}, f32[]{:T(128)}) all-reduce(f32[]{:T(128)S(6)} %mul.722, f32[]{:T(128)S(6)} %mul.729, f32[]{:T(128)S(6)} %mul.731), channel_id=1, replica_groups=mesh['row'=16,'col'=16] {'row','col'}, use_global_device_ids=true, to_apply=%region_19.20 | all-reduce | flops 3 | bytes 24 | tf_op jit(solution)/shard_map/psum | solution.py:122
  566.8 1.7 fusion.109
  568.6 1.0 while.208
  569.6 57.7 %psum.307 = f32[8192]{0:T(1024)S(1)} all-reduce(f32[8192]{0:T(1024)S(1)} %bitcast.322), channel_id=1, replica_groups=mesh['row'=16,'col'=16] {'col'}, use_global_device_ids=true, to_apply=%region_34.35 | all-reduce | flops 8192 | bytes 65536 | tf_op jit(solution)/shard_map/psum | solution.py:82
  628.0 1.0 fusion.107
  629.0 1.0 while.209
  630.0 56.1 %psum.309 = f32[8192]{0:T(1024)S(1)} all-reduce(f32[8192]{0:T(1024)S(1)} %bitcast.323), channel_id=1, replica_groups=mesh['row'=16,'col'=16] {'row'}, use_global_device_ids=true, to_apply=%region_39.40 | all-reduce | flops 8192 | bytes 65536 | tf_op jit(solution)/shard_map/psum | solution.py:88
  686.1 0.7 multiply_reduce_fusion.14
  688.8 74.0 %all-reduce.4 = (f32[]{:T(128)}, f32[]{:T(128)}, f32[]{:T(128)}) all-reduce(f32[]{:T(128)S(6)} %mul.736, f32[]{:T(128)S(6)} %mul.743, f32[]{:T(128)S(6)} %mul.745), channel_id=1, replica_groups=mesh['row'=16,'col'=16] {'row','col'}, use_global_device_ids=true, to_apply=%region_31.32 | all-reduce | flops 3 | bytes 24 | tf_op jit(solution)/shard_map/psum | solution.py:122
  765.7 1.7 fusion.105
  767.5 1.0 while.210
  768.5 57.7 %psum.312 = f32[8192]{0:T(1024)S(1)} all-reduce(f32[8192]{0:T(1024)S(1)} %bitcast.324), channel_id=1, replica_groups=mesh['row'=16,'col'=16] {'col'}, use_global_device_ids=true, to_apply=%region_46.47 | all-reduce | flops 8192 | bytes 65536 | tf_op jit(solution)/shard_map/psum | solution.py:82
  826.2 0.7 multiply_reduce_fusion.10
  827.0 1.0 fusion.103
  828.0 1.0 while.211
  829.6 1.0 fusion.101
  830.6 1.0 while.212
  832.5 1.7 fusion.97
  834.2 1.0 while.214
  837.7 103.5 %all-reduce.15.cloned.1.call-done = (f32[8192]{0:T(1024)}, f32[8192]{0:T(1024)}) async-done(((f32[8192]{0:T(1024)}, f32[8192]{0:T(1024)}), (f32[8192]{0:T(1024)}, f32[8192]{0:T(1024)})) %all-reduce.15.cloned.1.call-update) | async-done | bytes 65552 | tf_op jit(solution)/shard_map/psum | solution.py:88
  941.2 1.4 multiply_reduce_fusion.11
  943.9 76.9 %all-reduce.3 = (f32[]{:T(128)}, f32[]{:T(128)}, f32[]{:T(128)}, f32[]{:T(128)}, f32[]{:T(128)}) all-reduce(f32[]{:T(128)S(6)} %mul.750, f32[]{:T(128)S(6)} %mul.757, f32[]{:T(128)S(6)} %mul.759, f32[]{:T(128)S(6)} %mul.775, f32[]{:T(128)S(6)} %mul.778), channel_id=1, replica_groups=mesh['row'=16,'col'=16] {'row','col'}, use_global_device_ids=true, to_apply=%region_43.44 | all-reduce | flops 5 | bytes 40 | tf_op jit(solution)/shard_map/psum | solution.py:122
  1024.3 1.7 fusion.99
  1026.1 1.0 while.213
  1027.7 86.1 %all-reduce.13.cloned.1.call-done = (f32[8192]{0:T(1024)}, f32[8192]{0:T(1024)}) async-done(((f32[8192]{0:T(1024)}, f32[8192]{0:T(1024)}), (f32[8192]{0:T(1024)}, f32[8192]{0:T(1024)})) %all-reduce.13.cloned.1.call-update) | async-done | bytes 65552 | tf_op jit(solution)/shard_map/psum | solution.py:82
  1113.8 1.4 multiply_reduce_fusion.7
  1115.4 1.0 fusion.95
  1116.4 1.0 while.215
  1117.4 45.5 %psum.323 = f32[8192]{0:T(1024)S(1)} all-reduce(f32[8192]{0:T(1024)S(1)} %bitcast.329), channel_id=1, replica_groups=mesh['row'=16,'col'=16] {'row'}, use_global_device_ids=true, to_apply=%region_73.74 | all-reduce | flops 8192 | bytes 65536 | tf_op jit(solution)/shard_map/psum | solution.py:88
  1165.5 77.0 %all-reduce.2 = (f32[]{:T(128)}, f32[]{:T(128)}, f32[]{:T(128)}) all-reduce(f32[]{:T(128)S(6)} %mul.783, f32[]{:T(128)S(6)} %mul.790, f32[]{:T(128)S(6)} %mul.792), channel_id=1, replica_groups=mesh['row'=16,'col'=16] {'row','col'}, use_global_device_ids=true, to_apply=%region_62.63 | all-reduce | flops 3 | bytes 24 | tf_op jit(solution)/shard_map/psum | solution.py:122
  1244.8 1.7 fusion.93
  1246.6 1.0 while.216
  1247.6 56.9 %psum.326 = f32[8192]{0:T(1024)S(1)} all-reduce(f32[8192]{0:T(1024)S(1)} %bitcast.330), channel_id=1, replica_groups=mesh['row'=16,'col'=16] {'col'}, use_global_device_ids=true, to_apply=%region_80.81 | all-reduce | flops 8192 | bytes 65536 | tf_op jit(solution)/shard_map/psum | solution.py:82
  1305.3 1.0 fusion.91
  1306.3 1.0 while.217
  1307.3 56.9 %psum.328 = f32[8192]{0:T(1024)S(1)} all-reduce(f32[8192]{0:T(1024)S(1)} %bitcast.331), channel_id=1, replica_groups=mesh['row'=16,'col'=16] {'row'}, use_global_device_ids=true, to_apply=%region_85.86 | all-reduce | flops 8192 | bytes 65536 | tf_op jit(solution)/shard_map/psum | solution.py:88
  1366.8 75.0 %all-reduce.1 = (f32[]{:T(128)}, f32[]{:T(128)}, f32[]{:T(128)}) all-reduce(f32[]{:T(128)S(6)} %mul.799, f32[]{:T(128)S(6)} %mul.806, f32[]{:T(128)S(6)} %mul.808), channel_id=1, replica_groups=mesh['row'=16,'col'=16] {'row','col'}, use_global_device_ids=true, to_apply=%region_77.78 | all-reduce | flops 3 | bytes 24 | tf_op jit(solution)/shard_map/psum | solution.py:122
  1444.1 1.7 fusion.89
  1445.9 1.0 while.218
  1446.9 56.8 %psum.331 = f32[8192]{0:T(1024)S(1)} all-reduce(f32[8192]{0:T(1024)S(1)} %bitcast.332), channel_id=1, replica_groups=mesh['row'=16,'col'=16] {'col'}, use_global_device_ids=true, to_apply=%region_92.93 | all-reduce | flops 8192 | bytes 65536 | tf_op jit(solution)/shard_map/psum | solution.py:82
  1504.5 1.0 fusion.87
  1505.5 1.0 while.219
  1506.4 56.9 %psum.333 = f32[8192]{0:T(1024)S(1)} all-reduce(f32[8192]{0:T(1024)S(1)} %bitcast.333), channel_id=1, replica_groups=mesh['row'=16,'col'=16] {'row'}, use_global_device_ids=true, to_apply=%region_97.98 | all-reduce | flops 8192 | bytes 65536 | tf_op jit(solution)/shard_map/psum | solution.py:88
  1566.1 74.1 %all-reduce = (f32[]{:T(128)}, f32[]{:T(128)}, f32[]{:T(128)}) all-reduce(f32[]{:T(128)S(6)} %mul.815, f32[]{:T(128)S(6)} %mul.822, f32[]{:T(128)S(6)} %mul.824), channel_id=1, replica_groups=mesh['row'=16,'col'=16] {'row','col'}, use_global_device_ids=true, to_apply=%region_89.90 | all-reduce | flops 3 | bytes 24 | tf_op jit(solution)/shard_map/psum | solution.py:122
  1643.1 1.7 fusion.85
  1644.8 1.0 while.220
  1645.8 57.7 %psum.335 = f32[8192]{0:T(1024)S(1)} all-reduce(f32[8192]{0:T(1024)S(1)} %bitcast.317), channel_id=1, replica_groups=mesh['row'=16,'col'=16] {'col'}, use_global_device_ids=true, to_apply=%region_102.103 | all-reduce | flops 8192 | bytes 65536 | tf_op jit(solution)/shard_map/psum | solution.py:82
  (122 shorter events, 32.4 us)
Async XLA Ops:
  7.2 0.8 copy-start.1
  7.2 1.4 copy-start.2
  7.2 162.6 %copy-start = (f32[1,1,16,128,128]{4,3,2,1,0:T(8,128)S(1)}, f32[1,1,16,128,128]{4,3,2,1,0:T(8,128)}, u32[]{:S(2)}) copy-start(f32[1,1,16,128,128]{4,3,2,1,0:T(8,128)} %param.43) | copy-start | bytes 3145732
  7.2 934.0 %all-reduce.15.cloned.1.call-start = ((), (), s32[]{:S(2)}) async-start(), calls=%async_computation.1 | async-start | bytes 131072 | tf_op jit(solution)/shard_map/psum | solution.py:88
  93.3 75.7 %copy-start.3 = (f32[8192]{0:T(1024)S(1)}, f32[8192]{0:T(1024)}, u32[]{:S(2)}) copy-start(f32[8192]{0:T(1024)} %param.48) | copy-start | bytes 98308
  93.3 75.7 %copy-start.11 = (s32[8192]{0:T(1024)S(1)}, s32[8192]{0:T(1024)}, u32[]{:S(2)}) copy-start(s32[8192]{0:T(1024)} %param.49) | copy-start | bytes 98308
  169.0 0.7 copy-start.12
  171.6 0.7 copy-start.13
  173.2 56.8 %copy-start.10 = (s32[8192]{0:T(1024)S(1)}, s32[8192]{0:T(1024)}, u32[]{:S(2)}) copy-start(s32[8192]{0:T(1024)} %param.51) | copy-start | bytes 98308
  829.0 0.6 copy-start.4
  831.6 0.6 copy-start.5
  832.2 281.6 %all-reduce.13.cloned.1.call-start = ((), (), s32[]{:S(2)}) async-start(), calls=%async_computation | async-start | bytes 131072 | tf_op jit(solution)/shard_map/psum | solution.py:82
  835.2 0.6 copy-start.6
  942.6 81.5 %copy-start.8 = (f32[8192]{0:T(1024)S(1)}, f32[8192]{0:T(1024)}, u32[]{:S(2)}) copy-start(f32[8192]{0:T(1024)} %get-tuple-element.1828) | copy-start | bytes 98308
  1027.1 0.6 copy-start.7
  1247.6 56.9 %copy-start.9 = (f32[8192]{0:T(1024)S(1)}, f32[8192]{0:T(1024)}, u32[]{:S(2)}) copy-start(f32[8192]{0:T(1024)} %get-tuple-element.1827) | copy-start | bytes 98308
Sparse Core Ops, SparseCore 0:
  832.4 108.8 all-reduce.14
  1027.8 85.9 all-reduce.12
where the time goes:
time: 1730 us; the launch traced here: 1710 us
  blocking collectives  1410 us (82%)
  waiting for transfers between devices  190 us (11%)
  between operations  49.5 us (3%)
  matrix products  31.9 us (2%)
  other arithmetic  28 us (2%)
    psum x7, blocking collectives, per_device(): lax.psum((jnp.sum(primal_move * (next_col - col_image)) * primal_mask, jn...  525 us
    psum x7, blocking collectives, forward(): return lax.psum(partial_rows, 'col')  401 us
    psum x6, blocking collectives, backward(): return lax.psum(partial_cols, 'row')  328 us
    psum x1, waiting for transfers between devices, backward(): return lax.psum(partial_cols, 'row')  103 us
    psum x1, waiting for transfers between devices, forward(): return lax.psum(partial_rows, 'col')  86.1 us
    psum x1, blocking collectives, pair_sums(): lax.psum((primal_term * primal_mask, dual_term * dual_mask), ('row', 'col'))  81.4 us
    pmax x1, blocking collectives, per_device(): largest = lax.pmax(local_largest, ('row', 'col'))  72.7 us
  transfers between devices with their start and end apart: 2, of which 2 were waited for; matrix products, arithmetic and copies ran while one was open for 0% of the time, Pallas kernels for 0%

commit v1 on v0

v1 whole, which is shorter than its diff:
```python
import functools

import jax
import jax.numpy as jnp
from jax import lax
from jax.experimental import pallas as pl
from jax.experimental.pallas import tpu as pltpu
from jax.sharding import PartitionSpec as P

MESH = pl.DeviceIdType.MESH
TILE = 128
SLOTS = 16
GRID = 64
FULL = GRID + SLOTS
OUTER = 2
INNER = 4
STEPS = OUTER * INNER
GROUP = 16
MSG = SLOTS + 8
PAIRS = SLOTS // 2
F32 = jnp.float32
BF16 = jnp.bfloat16


def split3(x):
    hi = x.astype(BF16)
    rest = x - hi.astype(F32)
    mid = rest.astype(BF16)
    lo = (rest - mid.astype(F32)).astype(BF16)
    return hi, mid, lo


def total(x):
    return jnp.sum(jnp.sum(x, axis=0, keepdims=True), axis=1, keepdims=True)


def lane_sums(x):
    return jnp.sum(x, axis=0, keepdims=True)


def col_peers(row, col):
    x, y = col // 4, col % 4
    offsets = [(dx, dy) for dx in range(4) for dy in range(4) if dx or dy]
    offsets.sort(key=lambda o: -(min(o[0], 4 - o[0]) + min(o[1], 4 - o[1])))
    return [(row, ((x + dx) % 4) * 4 + (y + dy) % 4) for dx, dy in offsets]


def row_peers(row, col):
    z, core = row // 2, row % 2
    offsets = [(dz, dc) for dz in range(8) for dc in range(2) if dz or dc]
    offsets.sort(key=lambda o: -(min(o[0], 8 - o[0]) * 2 + o[1]))
    return [(((z + dz) % 8) * 2 + (core + dc) % 2, col) for dz, dc in offsets]


def kernel(
    tiles_hbm, slot_rows, slot_cols, counts, objective, upper, bound_codes, rhs, row_codes,
    primal_out, dual_out,
    tiles, w_forward, w_backward, sum_forward, sum_backward,
    obj, lower, higher, right, floor,
    s_primal, s_dual, s_rows, s_cols, t_primal, t_dual, t_rows, t_cols, b_primal, b_dual,
    scalars, col_buf, row_buf, col_start, row_start,
    tile_sem, col_send, col_recv, row_send, row_recv, start_sem,
):
    row, col = lax.axis_index("row"), lax.axis_index("col")
    live = counts[0]
    fetch = pltpu.make_async_copy(tiles_hbm, tiles, tile_sem)
    fetch.start()

    by_col, by_row = col_peers(row, col), row_peers(row, col)
    barrier = pltpu.get_barrier_semaphore()
    for peer in by_col + by_row:
        pl.semaphore_signal(barrier, inc=1, device_id=peer, device_id_type=MESH)

    def exchange(slots, me, peers, send, recv):
        mine = slots.at[me]
        for peer in peers:
            pltpu.make_async_remote_copy(
                src_ref=mine, dst_ref=mine, send_sem=send, recv_sem=recv,
                device_id=peer, device_id_type=MESH,
            ).start()

    def arrive(slots, send, recv):
        others = slots.at[pl.ds(0, GROUP - 1)]
        pltpu.make_async_copy(others, others, recv).wait()
        pltpu.make_async_copy(others, others, send).wait()

    def widen(dst, src, indices):
        dst[0:GRID, :] = src[...]
        for t in range(SLOTS):
            dst[GRID + t : GRID + t + 1, :] = src[pl.ds(indices[t], 1), :]

    widen(obj, objective, slot_cols)
    widen(right, rhs, slot_rows)
    infinity = jnp.inf
    lower[0:GRID, :] = jnp.where(bound_codes[...] >= 1, 0.0, -infinity)
    higher[0:GRID, :] = jnp.where(bound_codes[...] == 2, upper[...], infinity)
    floor[0:GRID, :] = jnp.where(row_codes[...] == 1, 0.0, -infinity)
    for t in range(SLOTS):
        at = slice(GRID + t, GRID + t + 1)
        code = bound_codes[pl.ds(slot_cols[t], 1), :]
        lower[at, :] = jnp.where(code >= 1, 0.0, -infinity)
        higher[at, :] = jnp.where(code == 2, upper[pl.ds(slot_cols[t], 1), :], infinity)
        floor[at, :] = jnp.where(row_codes[pl.ds(slot_rows[t], 1), :] == 1, 0.0, -infinity)

    rows8 = lax.broadcasted_iota(jnp.int32, (8, TILE), 0)
    lanes8 = lax.broadcasted_iota(jnp.int32, (8, TILE), 1)
    entry = rows8 * TILE + lanes8

    def index_tile(indices, me):
        placed = jnp.zeros((8, TILE), F32)
        for t in range(SLOTS):
            placed = jnp.where(entry == me * SLOTS + t, indices[t].astype(F32), placed)
        return placed

    def slot_column(indices):
        column = jnp.zeros((SLOTS, 2 * TILE), F32)
        which = lax.broadcasted_iota(jnp.int32, (SLOTS, 2 * TILE), 0)
        for t in range(SLOTS):
            column = jnp.where(which == t, indices[t].astype(F32), column)
        return column

    def sum_matrix(dst, summed, indices):
        entries = jnp.concatenate([summed[0:1, :], summed[1:2, :]], axis=1)
        block = lax.broadcasted_iota(jnp.int32, (GRID, 2 * TILE), 0).astype(F32)
        dst[0:GRID, :] = jnp.where(block == entries, 1.0, 0.0).astype(BF16)
        dst[GRID:FULL, :] = jnp.where(slot_column(indices) == entries, 1.0, 0.0).astype(BF16)

    fetch.wait()
    largest = jnp.zeros((8, TILE), F32)
    for t in range(SLOTS):
        tile = jnp.where(t < live, tiles[t], 0.0)
        tiles[t] = tile
        largest = jnp.maximum(largest, jnp.max(jnp.abs(tile).reshape(16, 8, TILE), axis=0))

    row_start[row] = jnp.where(
        rows8 < 2,
        index_tile(slot_cols, row),
        jnp.where(
            rows8 == 2,
            jnp.max(largest, axis=0, keepdims=True),
            jnp.where(rows8 == 3, lane_sums(rhs[...] * rhs[...]), 0.0),
        ),
    )
    pl.semaphore_wait(barrier, 2 * (GROUP - 1))
    exchange(row_start, row, by_row, start_sem.at[0], start_sem.at[1])

    for t in range(SLOTS):
        tile = tiles[t]
        at = slice(TILE * (t % 2), TILE * (t % 2) + TILE)
        for weights, block in ((w_backward, tile), (w_forward, tile.T)):
            hi = block.astype(BF16)
            weights[t // 2, 0:TILE, at] = hi
            weights[t // 2, TILE : 2 * TILE, at] = (block - hi.astype(F32)).astype(BF16)
    for state in (s_primal, s_dual, s_rows, s_cols, t_primal, t_dual, t_rows, t_cols, b_primal, b_dual):
        state[...] = jnp.zeros_like(state)

    arrive(row_start, start_sem.at[0], start_sem.at[1])
    got = row_start[...]
    summed = jnp.sum(got, axis=0)
    most = jnp.max(jnp.max(got, axis=0)[2:3, :], axis=1, keepdims=True)
    right_sq = jnp.sum(summed[3:4, :], axis=1, keepdims=True)
    col_start[col] = jnp.where(
        rows8 < 2,
        index_tile(slot_rows, col),
        jnp.where(
            rows8 == 2, most, jnp.where(rows8 == 3, lane_sums(objective[...] * objective[...]), 0.0)
        ),
    )
    exchange(col_start, col, by_col, start_sem.at[2], start_sem.at[3])
    sum_matrix(sum_backward, summed, slot_cols)
    arrive(col_start, start_sem.at[2], start_sem.at[3])
    got = col_start[...]
    summed = jnp.sum(got, axis=0)
    sum_matrix(sum_forward, summed, slot_rows)
    most = jnp.max(jnp.max(got, axis=0)[2:3, :], axis=1, keepdims=True)
    object_sq = jnp.sum(summed[3:4, :], axis=1, keepdims=True)
    ones = jnp.ones((1, TILE), F32)
    scalars[0:1, :] = 0.05 / (most + 1e-06) * ones
    scalars[1:2, :] = jnp.sqrt((object_sq + 1e-06) / (right_sq + 1e-06)) * ones
    scalars[2:3, :] = jnp.zeros((1, TILE), F32)

    def images(weights, pieces):
        stacked = jnp.concatenate(split3(pieces), axis=0)
        operand = jnp.concatenate([stacked, stacked], axis=1)
        which = lax.broadcasted_iota(jnp.int32, (8, TILE), 0)
        halves = [jnp.zeros((8, TILE), F32), jnp.zeros((8, TILE), F32)]
        for pair in range(PAIRS):
            product = jnp.dot(operand, weights[pair], preferred_element_type=F32)
            half, first = pair // 4, 2 * pair % 8
            base = 8 * half
            both = sum(product[base + SLOTS * s : base + SLOTS * s + 8, :] for s in range(3))
            halves[half] = jnp.where(which == first, both[:, 0:TILE], halves[half])
            halves[half] = jnp.where(which == first + 1, both[:, TILE : 2 * TILE], halves[half])
        return halves

    def summed_rows(matrix, slots):
        data = slots[:, 0:SLOTS, :].reshape(GROUP * SLOTS, TILE)
        ones_at = matrix[...]
        return sum(jnp.dot(ones_at, part, preferred_element_type=F32) for part in split3(data))

    def post(slots, me, halves, sums):
        slots[me, 0:8, :] = halves[0]
        slots[me, 8:SLOTS, :] = halves[1]
        tile = jnp.zeros((8, TILE), F32)
        for i, value in enumerate(sums):
            tile = jnp.where(rows8 == i, value, tile)
        slots[me, SLOTS:MSG, :] = tile

    def gathered_sums(slots, number):
        tiles_in = jnp.sum(slots[:, SLOTS:MSG, :], axis=0)
        lanes = jnp.sum(tiles_in, axis=1, keepdims=True)
        return [lanes[i : i + 1, :] for i in range(number)]

    def iteration(k, _):
        parity = lax.rem(k, 2)
        last = k == STEPS - 1
        restart = k == INNER - 1
        step, weight = scalars[0:1, :], scalars[1:2, :]
        weight_total = scalars[2:3, :] + step
        primal = s_primal[...]
        next_primal = jnp.minimum(
            jnp.maximum(primal - step / weight * (obj[...] - s_cols[...]), lower[...]), higher[...]
        )
        halves = images(w_forward, next_primal[GRID:FULL, :])
        total_primal = t_primal[...] + step * next_primal
        mean_primal = total_primal / weight_total
        move = (next_primal - primal)[0:GRID, :]
        drift = (mean_primal - b_primal[...])[0:GRID, :]
        slots = col_buf.at[parity]
        post(slots, col, halves, (lane_sums(move * move), lane_sums(drift * drift)))
        exchange(slots, col, by_col, col_send, col_recv.at[parity])
        s_primal[...] = jnp.where(restart, mean_primal, next_primal)
        t_primal[...] = jnp.where(restart, 0.0, total_primal)
        b_primal[...] = jnp.where(restart, mean_primal, b_primal[...])

        @pl.when(last)
        def _():
            primal_out[...] = mean_primal[0:GRID, :]

        arrive(slots, col_send, col_recv.at[parity])
        next_rows = summed_rows(sum_forward, slots)
        primal_sq, primal_drift = gathered_sums(slots, 2)
        rows = s_rows[...]
        dual = s_dual[...]
        next_dual = jnp.maximum(
            dual + step * weight * (right[...] - (2.0 * next_rows - rows)), floor[...]
        )
        total_dual = t_dual[...] + step * next_dual
        mean_dual = total_dual / weight_total

        @pl.when(last)
        def _():
            dual_out[...] = mean_dual[0:GRID, :]

        @pl.when(jnp.logical_not(last))
        def _():
            halves = images(w_backward, next_dual[GRID:FULL, :])
            move = (next_dual - dual)[0:GRID, :]
            image_move = (next_rows - rows)[0:GRID, :]
            drift = (mean_dual - b_dual[...])[0:GRID, :]
            slots = row_buf.at[parity]
            post(
                slots, row, halves,
                (lane_sums(move * move), lane_sums(move * image_move), lane_sums(drift * drift)),
            )
            exchange(slots, row, by_row, row_send, row_recv.at[parity])
            total_rows = t_rows[...] + step * next_rows
            s_dual[...] = jnp.where(restart, mean_dual, next_dual)
            t_dual[...] = jnp.where(restart, 0.0, total_dual)
            b_dual[...] = jnp.where(restart, mean_dual, b_dual[...])
            s_rows[...] = jnp.where(restart, total_rows / weight_total, next_rows)
            t_rows[...] = jnp.where(restart, 0.0, total_rows)

            shrink, growth = jnp.float32(0.0), jnp.float32(0.0)
            for i in range(STEPS - 1):
                shrink = jnp.where(k == i, jnp.float32(1.0 - (i + 2) ** (-0.3)), shrink)
                growth = jnp.where(k == i, jnp.float32(1.0 + (i + 2) ** (-0.6)), growth)

            arrive(slots, row_send, row_recv.at[parity])
            next_cols = summed_rows(sum_backward, slots)
            dual_sq, inter, dual_drift = gathered_sums(slots, 3)
            numer = shrink * (weight * primal_sq + dual_sq / weight + 1e-06)
            new_step = numer / jnp.maximum(2.0 * jnp.abs(inter), numer / (growth * step))
            new_weight = jnp.sqrt(
                weight * jnp.sqrt(dual_drift + 1e-06) / jnp.sqrt(primal_drift + 1e-06)
            )
            total_cols = t_cols[...] + step * next_cols
            s_cols[...] = jnp.where(restart, total_cols / weight_total, next_cols)
            t_cols[...] = jnp.where(restart, 0.0, total_cols)
            scalars[0:1, :] = new_step
            scalars[1:2, :] = jnp.where(restart, new_weight, weight)
            scalars[2:3, :] = jnp.where(restart, 0.0, weight_total)

        return 0

    lax.fori_loop(0, STEPS, iteration, 0)


def per_device(
    tiles, tile_rows, tile_cols, tile_counts, objective, upper, bound_codes, rhs, row_codes
):
    vector = lambda: pltpu.VMEM((FULL, TILE), F32)
    blocked = lambda v: v.reshape(GRID, TILE)
    smem = pl.BlockSpec(memory_space=pltpu.SMEM)
    vmem = pl.BlockSpec(memory_space=pltpu.VMEM)
    primal, dual = pl.pallas_call(
        kernel,
        out_shape=(jax.ShapeDtypeStruct((GRID, TILE), F32),) * 2,
        in_specs=[pl.BlockSpec(memory_space=pl.ANY), smem, smem, smem] + [vmem] * 5,
        out_specs=(vmem, vmem),
        scratch_shapes=[
            pltpu.VMEM((SLOTS, TILE, TILE), F32),
            pltpu.VMEM((PAIRS, 2 * TILE, 2 * TILE), BF16),
            pltpu.VMEM((PAIRS, 2 * TILE, 2 * TILE), BF16),
            pltpu.VMEM((FULL, 2 * TILE), BF16),
            pltpu.VMEM((FULL, 2 * TILE), BF16),
        ]
        + [vector() for _ in range(15)]
        + [
            pltpu.VMEM((8, TILE), F32),
            pltpu.VMEM((2, GROUP, MSG, TILE), F32),
            pltpu.VMEM((2, GROUP, MSG, TILE), F32),
            pltpu.VMEM((GROUP, 8, TILE), F32),
            pltpu.VMEM((GROUP, 8, TILE), F32),
            pltpu.SemaphoreType.DMA,
            pltpu.SemaphoreType.DMA,
            pltpu.SemaphoreType.DMA((2,)),
            pltpu.SemaphoreType.DMA,
            pltpu.SemaphoreType.DMA((2,)),
            pltpu.SemaphoreType.DMA((4,)),
        ],
        compiler_params=pltpu.CompilerParams(collective_id=0, has_side_effects=True),
        name="pdlp",
    )(
        tiles.reshape(SLOTS, TILE, TILE),
        tile_rows.reshape(SLOTS),
        tile_cols.reshape(SLOTS),
        tile_counts.reshape(1),
        blocked(objective),
        blocked(upper),
        blocked(bound_codes),
        blocked(rhs),
        blocked(row_codes),
    )
    return primal.reshape(-1), dual.reshape(-1)


def solution(mesh):
    placed = (
        P("row", "col", None, None, None),
        P("row", "col", None),
        P("row", "col", None),
        P("row", "col"),
        P("col"),
        P("col"),
        P("col"),
        P("row"),
        P("row"),
    )
    return jax.shard_map(
        per_device, mesh=mesh, in_specs=placed, out_specs=(P("col"), P("row")), check_vma=False
    )
```

time: 1730 us -> 113 us (0.07); the launches traced: 1710 us -> 113 us
  blocking collectives: 1410 us -> 0 us
  waiting for transfers between devices: 190 us -> 0 us
  Pallas kernels: 0 us -> 110 us
  between operations: 49.5 us -> 1.29 us
  matrix products: 31.9 us -> 0 us
  other arithmetic: 28 us -> 0 us
    psum x21 -> x0, blocking collectives: 1340 us -> none  [the longest x7 525 us: per_device(): lax.psum((jnp.sum(primal_move * (next_col - col_image)) * primal_mask, jn...]
    psum x2 -> x0, waiting for transfers between devices: 190 us -> none  [the longest x1 103 us: backward(): return lax.psum(partial_cols, 'row')]
    pallas_call x0 -> x1, Pallas kernels: none -> 110 us  [per_device(): pl.pallas_call(kernel, out_shape=(jax.ShapeDtypeStruct((GRID, TILE), F32)...]
    pmax x1 -> x0, blocking collectives: 72.7 us -> none  [per_device(): largest = lax.pmax(local_largest, ('row', 'col'))]
    dot_general x51 -> x0, matrix products: 31.9 us -> none  [the longest x9 15.7 us: visit(): images = jnp.einsum('tij,tj->ti', tile_data, pieces, precision=highest)]
  transfers between devices with their start and end apart: 2 -> 0, of which waited for: 2 -> 0; matrix products, arithmetic and copies ran while one was open for 0% -> 0% of each run, Pallas kernels for 0% -> 0%
where the time goes in v1:
time: 113 us
  Pallas kernels  110 us (97%)
  local copies, waits for them, and re-layouts  2 us (2%)
  between operations  1.29 us (1%)
    pallas_call x1, Pallas kernels, per_device(): pl.pallas_call(kernel, out_shape=(jax.ShapeDtypeStruct((GRID, TILE), F32)...  110 us

profile of v1, /device:TPU:1, one launch (start us, length us, event | category | flops | bytes accessed | tf_op | source)
XLA Modules:
  0.0 113.1 jit_solution(17426333233355631177)
XLA Ops:
  1.3 109.8 %pdlp.1 = (f32[64,128]{1,0:T(8,128)}, f32[64,128]{1,0:T(8,128)}) custom-call(f32[16,128,128]{2,1,0:T(8,128)} %bitcast.12, s32[16]{0:T(128)} %bitcast.20, s32[16]{0:T(128)} %bitcast.21, s32[1]{0:T(128)} %bitcast.11.counts, f32[64,128]{1,0:T(8,128)} %bitcast.13, f32[64,128]{1,0:T(8,128)} %bitcast.14, s32[64,128]{1,0:T(8,128)} %bitcast.15, f32[64,128]{1,0:T(8,128)} %bitcast.16, ...), custom_call_target="tpu_custom_call" | custom-call | tf_op jit(solution)/shard_map/pdlp/pallas_call | solution.py:306
  111.0 0.0 copy-start
  111.1 1.4 %copy.14 = f32[8192]{0:T(1024)} copy(f32[8192]{0:T(1024)} %bitcast.19) | data formatting | bytes 65536
  112.4 0.0 copy-done
  112.4 0.6 copy.15
Async XLA Ops:
  111.0 1.4 %copy-start = (f32[64,128]{1,0:T(8,128)S(1)}, f32[64,128]{1,0:T(8,128)}, u32[]{:S(2)}) copy-start(f32[64,128]{1,0:T(8,128)} %get-tuple-element.5) | copy-start | bytes 98308

commit v2 on v1

v2 whole, which is shorter than its diff:
```python
import jax
import jax.numpy as jnp
from jax import lax
from jax.experimental import pallas as pl
from jax.experimental.pallas import tpu as pltpu
from jax.sharding import PartitionSpec as P

MESH = pl.DeviceIdType.MESH
TILE = 128
SLOTS = 16
GRID = 64
FULL = GRID + SLOTS
OUTER = 2
INNER = 4
STEPS = OUTER * INNER
GROUP = 16
CHIPS = 8
MSG = SLOTS + 1
ROOM = 24
BOTH = FULL + 1
PAIRS = SLOTS // 2
START = 3
F32 = jnp.float32
BF16 = jnp.bfloat16


def split3(x):
    hi = x.astype(BF16)
    rest = x - hi.astype(F32)
    mid = rest.astype(BF16)
    lo = (rest - mid.astype(F32)).astype(BF16)
    return hi, mid, lo


def total(x):
    return jnp.sum(jnp.sum(x, axis=0, keepdims=True), axis=1, keepdims=True)


def col_peers(row, col):
    x, y = col // 4, col % 4
    offsets = [(dx, dy) for dx in range(4) for dy in range(4) if dx or dy]
    offsets.sort(key=lambda o: -(min(o[0], 4 - o[0]) + min(o[1], 4 - o[1])))
    return [(row, ((x + dx) % 4) * 4 + (y + dy) % 4) for dx, dy in offsets]


def row_peers(row, col, cores):
    z, core = row // 2, row % 2
    offsets = [(dz, dc) for dz in range(CHIPS) for dc in range(cores) if dz or dc]
    offsets.sort(key=lambda o: -(min(o[0], CHIPS - o[0]) * 2 + o[1]))
    return [(((z + dz) % CHIPS) * 2 + (core + dc) % 2, col) for dz, dc in offsets]


def kernel(
    tiles_hbm, slot_rows_hbm, slot_cols_hbm, counts_hbm, objective_hbm, upper_hbm, bound_hbm, rhs_hbm, codes_hbm,
    primal_out, dual_out,
    tiles, slot_rows, slot_cols, counts, objective, upper, bound_codes, rhs, row_codes,
    w_forward, w_backward, sum_forward, sum_backward,
    obj, lower, higher, right, floor,
    s_primal, s_dual, s_rows, s_cols, t_primal, t_dual, t_rows, t_cols, b_primal, b_dual,
    scalars, col_buf, row_buf, core_out, core_in, col_start, row_start, my_slots, its_slots,
    fetch_sem, col_send, col_recv, row_send, row_recv, core_send, core_recv, start_sem,
):
    row, col = lax.axis_index("row"), lax.axis_index("col")
    chip, core = row // 2, row % 2
    by_col, by_row = col_peers(row, col), row_peers(row, col, 2)
    by_chip = row_peers(row, col, 1)
    sibling = (chip * 2 + (core + 1) % 2, col)
    barrier = pltpu.get_barrier_semaphore()
    for peer in by_col + by_row:
        pl.semaphore_signal(barrier, inc=1, device_id=peer, device_id_type=MESH)
    fetches = [
        pltpu.make_async_copy(src, dst, fetch_sem.at[i])
        for i, (src, dst) in enumerate((
            (counts_hbm, counts), (slot_rows_hbm, slot_rows), (slot_cols_hbm, slot_cols), (tiles_hbm, tiles),
            (rhs_hbm, rhs), (objective_hbm, objective), (upper_hbm, upper), (bound_hbm, bound_codes),
            (codes_hbm, row_codes),
        ))
    ]
    for fetch in fetches:
        fetch.start()

    def send_to(src, dst, peer, send, recv):
        pltpu.make_async_remote_copy(
            src_ref=src, dst_ref=dst, send_sem=send, recv_sem=recv,
            device_id=peer, device_id_type=MESH,
        ).start()

    def exchange(slots, me, rows, peers, send, recv):
        mine = slots.at[me, 0:rows]
        for peer in peers:
            send_to(mine, mine, peer, send, recv)

    def wait_for(shape, sem):
        pltpu.make_async_copy(shape, shape, sem).wait()

    def arrive(slots, rows, number, send, recv):
        others = slots.at[pl.ds(0, number), 0:rows]
        wait_for(others, recv)
        wait_for(others, send)

    ones = jnp.ones((1, TILE), F32)
    lane = lax.broadcasted_iota(jnp.int32, (1, TILE), 1)
    for state in (s_primal, s_dual, s_rows, s_cols, t_primal, t_dual, t_rows, t_cols, b_primal, b_dual):
        state[...] = jnp.zeros_like(state)
    for fetch in fetches:
        fetch.wait()

    live = counts[0]
    largest = jnp.zeros((8, TILE), F32)
    for t in range(SLOTS):
        size = jnp.max(jnp.abs(tiles[t]).reshape(16, 8, TILE), axis=0)
        largest = jnp.where(t < live, jnp.maximum(largest, size), largest)

    def index_row(indices, first):
        placed = jnp.zeros((1, TILE), F32)
        for t in range(SLOTS):
            placed = jnp.where(lane == first + t, indices[t].astype(F32), placed)
        return placed

    def slot_column(indices):
        which = lax.broadcasted_iota(jnp.int32, (SLOTS, TILE), 0)
        column = jnp.zeros((SLOTS, TILE), F32)
        for t in range(SLOTS):
            column = jnp.where(which == t, indices[t].astype(F32), column)
        return column

    row_start[row, 0:1, :] = index_row(slot_cols, chip * SLOTS)
    row_start[row, 1:2, :] = jnp.where(
        lane == 0,
        jnp.max(jnp.max(largest, axis=0, keepdims=True), axis=1, keepdims=True),
        total(rhs[...] * rhs[...]),
    )
    my_slots[...] = slot_column(slot_cols)
    pl.semaphore_wait(barrier, 2 * (GROUP - 1))
    exchange(row_start, row, 2, by_row, start_sem.at[0], start_sem.at[1])
    send_to(my_slots, its_slots, sibling, start_sem.at[4], start_sem.at[5])

    for t in range(SLOTS):
        tile = jnp.where(t < live, tiles[t], 0.0)
        at = slice(TILE * (t % 2), TILE * (t % 2) + TILE)
        for weights, block in ((w_backward, tile), (w_forward, tile.T)):
            hi = block.astype(BF16)
            weights[t // 2, 0:TILE, at] = hi
            weights[t // 2, TILE : 2 * TILE, at] = (block - hi.astype(F32)).astype(BF16)

    infinity = jnp.inf
    obj[0:GRID, :] = objective[...]
    right[0:GRID, :] = rhs[...]
    lower[0:GRID, :] = jnp.where(bound_codes[...] >= 1, 0.0, -infinity)
    higher[0:GRID, :] = jnp.where(bound_codes[...] == 2, upper[...], infinity)
    floor[0:GRID, :] = jnp.where(row_codes[...] == 1, 0.0, -infinity)
    for t in range(SLOTS):
        at = slice(GRID + t, GRID + t + 1)
        i, j = pl.ds(slot_rows[t], 1), pl.ds(slot_cols[t], 1)
        obj[at, :] = objective[j, :]
        right[at, :] = rhs[i, :]
        lower[at, :] = jnp.where(bound_codes[j, :] >= 1, 0.0, -infinity)
        higher[at, :] = jnp.where(bound_codes[j, :] == 2, upper[j, :], infinity)
        floor[at, :] = jnp.where(row_codes[i, :] == 1, 0.0, -infinity)

    half = col // CHIPS
    at_rows = index_row(slot_rows, (col % CHIPS) * SLOTS)
    col_start[col, 0:1, :] = jnp.where(half == 0, at_rows, 0.0)
    col_start[col, 1:2, :] = jnp.where(half == 1, at_rows, 0.0)
    object_part = total(objective[...] * objective[...])

    arrive(row_start, 2, GROUP - 1, start_sem.at[0], start_sem.at[1])
    parts = row_start[:, 1, :]
    most = jnp.max(parts, axis=0, keepdims=True)[:, 0:1]
    right_sq = jnp.sum(parts, axis=0, keepdims=True)[:, 1:2]
    col_start[col, 2:3, :] = jnp.where(lane == 0, most, object_part)
    exchange(col_start, col, START, by_col, start_sem.at[2], start_sem.at[3])

    def one_hot(wanted, entries):
        return jnp.where(wanted == entries, 1.0, 0.0).astype(BF16)

    wait_for(its_slots, start_sem.at[5])
    wait_for(my_slots, start_sem.at[4])
    block = lax.broadcasted_iota(jnp.int32, (GRID, TILE), 0).astype(F32)
    entries = sum(
        jnp.where(core == n % 2, row_start[n, 0:1, :], 0.0) for n in range(GROUP)
    )
    sum_backward[0:GRID, :] = one_hot(block, entries)
    sum_backward[GRID:FULL, :] = one_hot(my_slots[...], entries)
    sum_backward[FULL : FULL + SLOTS, :] = one_hot(its_slots[...], entries)
    at_slots = slot_column(slot_rows)

    arrive(col_start, START, GROUP - 1, start_sem.at[2], start_sem.at[3])
    parts = col_start[:, 2, :]
    most = jnp.max(parts, axis=0, keepdims=True)[:, 0:1]
    object_sq = jnp.sum(parts, axis=0, keepdims=True)[:, 1:2]
    scalars[0:1, :] = 0.05 / (most + 1e-06) * ones
    scalars[1:2, :] = jnp.sqrt((object_sq + 1e-06) / (right_sq + 1e-06)) * ones
    scalars[2:3, :] = jnp.zeros((1, TILE), F32)
    for n in range(2):
        entries = jnp.sum(col_start[:, n, :], axis=0, keepdims=True)
        at = slice(n * TILE, n * TILE + TILE)
        sum_forward[0:GRID, at] = one_hot(block, entries)
        sum_forward[GRID:FULL, at] = one_hot(at_slots, entries)

    def images(weights, pieces):
        stacked = jnp.concatenate(split3(pieces), axis=0)
        operand = jnp.concatenate([stacked, stacked], axis=1)
        which = lax.broadcasted_iota(jnp.int32, (8, TILE), 0)
        halves = [jnp.zeros((8, TILE), F32), jnp.zeros((8, TILE), F32)]
        for pair in range(PAIRS):
            product = jnp.dot(operand, weights[pair], preferred_element_type=F32)
            side, first = pair // 4, 2 * pair % 8
            base = 8 * side
            both = sum(product[base + SLOTS * s : base + SLOTS * s + 8, :] for s in range(3))
            halves[side] = jnp.where(which == first, both[:, 0:TILE], halves[side])
            halves[side] = jnp.where(which == first + 1, both[:, TILE : 2 * TILE], halves[side])
        return halves

    def summed_rows(matrix, slots):
        data = slots[:, 0:SLOTS, :].reshape(-1, TILE)
        ones_at = matrix[...]
        return sum(jnp.dot(ones_at, part, preferred_element_type=F32) for part in split3(data))

    def post(slots, me, halves, sums):
        slots[me, 0:8, :] = halves[0]
        slots[me, 8:SLOTS, :] = halves[1]
        lanes = jnp.zeros((1, TILE), F32)
        for i, value in enumerate(sums):
            lanes = jnp.where(lane == i, value, lanes)
        slots[me, SLOTS:MSG, :] = lanes

    def gathered_sums(slots):
        return jnp.sum(slots[:, SLOTS, :], axis=0, keepdims=True)

    def iteration(k, _):
        parity = lax.rem(k, 2)
        last = k == STEPS - 1
        restart = k == INNER - 1
        step, weight = scalars[0:1, :], scalars[1:2, :]
        weight_total = scalars[2:3, :] + step
        primal = s_primal[...]
        next_primal = jnp.minimum(
            jnp.maximum(primal - step / weight * (obj[...] - s_cols[...]), lower[...]), higher[...]
        )
        halves = images(w_forward, next_primal[GRID:FULL, :])
        total_primal = t_primal[...] + step * next_primal
        mean_primal = total_primal / weight_total
        move = (next_primal - primal)[0:GRID, :]
        drift = (mean_primal - b_primal[...])[0:GRID, :]
        slots = col_buf.at[parity]
        post(slots, col, halves, (total(move * move), total(drift * drift)))
        exchange(slots, col, MSG, by_col, col_send, col_recv.at[parity])
        s_primal[...] = jnp.where(restart, mean_primal, next_primal)
        t_primal[...] = jnp.where(restart, 0.0, total_primal)
        b_primal[...] = jnp.where(restart, mean_primal, b_primal[...])

        @pl.when(last)
        def _():
            primal_out[...] = mean_primal[0:GRID, :]

        arrive(slots, MSG, GROUP - 1, col_send, col_recv.at[parity])
        next_rows = summed_rows(sum_forward, slots)
        sums = gathered_sums(slots)
        primal_sq, primal_drift = sums[:, 0:1], sums[:, 1:2]
        rows = s_rows[...]
        dual = s_dual[...]
        next_dual = jnp.maximum(
            dual + step * weight * (right[...] - (2.0 * next_rows - rows)), floor[...]
        )
        total_dual = t_dual[...] + step * next_dual
        mean_dual = total_dual / weight_total

        @pl.when(last)
        def _():
            dual_out[...] = mean_dual[0:GRID, :]

        @pl.when(jnp.logical_not(last))
        def _():
            halves = images(w_backward, next_dual[GRID:FULL, :])
            move = (next_dual - dual)[0:GRID, :]
            image_move = (next_rows - rows)[0:GRID, :]
            drift = (mean_dual - b_dual[...])[0:GRID, :]
            slots = row_buf.at[parity]
            post(slots, chip, halves, (total(move * move), total(move * image_move), total(drift * drift)))
            exchange(slots, chip, MSG, by_chip, row_send, row_recv.at[parity])
            total_rows = t_rows[...] + step * next_rows
            s_dual[...] = jnp.where(restart, mean_dual, next_dual)
            t_dual[...] = jnp.where(restart, 0.0, total_dual)
            b_dual[...] = jnp.where(restart, mean_dual, b_dual[...])
            s_rows[...] = jnp.where(restart, total_rows / weight_total, next_rows)
            t_rows[...] = jnp.where(restart, 0.0, total_rows)

            shrink, growth = jnp.float32(0.0), jnp.float32(0.0)
            for i in range(STEPS - 1):
                shrink = jnp.where(k == i, jnp.float32(1.0 - (i + 2) ** (-0.3)), shrink)
                growth = jnp.where(k == i, jnp.float32(1.0 + (i + 2) ** (-0.6)), growth)

            arrive(slots, MSG, CHIPS - 1, row_send, row_recv.at[parity])
            mine = summed_rows(sum_backward, slots)
            sums = gathered_sums(slots)
            core_out[0:GRID, :] = mine[0:GRID, :]
            core_out[GRID:FULL, :] = mine[FULL : FULL + SLOTS, :]
            core_out[FULL:BOTH, :] = sums
            outgoing, incoming = core_out.at[0:BOTH], core_in.at[parity, 0:BOTH]
            send_to(outgoing, incoming, sibling, core_send, core_recv.at[parity])
            wait_for(incoming, core_recv.at[parity])
            wait_for(outgoing, core_send)
            next_cols = mine[0:FULL, :] + core_in[parity, 0:FULL, :]
            sums = sums + core_in[parity, FULL:BOTH, :]
            dual_sq, inter, dual_drift = sums[:, 0:1], sums[:, 1:2], sums[:, 2:3]
            numer = shrink * (weight * primal_sq + dual_sq / weight + 1e-06)
            new_step = numer / jnp.maximum(2.0 * jnp.abs(inter), numer / (growth * step))
            new_weight = jnp.sqrt(
                weight * jnp.sqrt(dual_drift + 1e-06) / jnp.sqrt(primal_drift + 1e-06)
            )
            total_cols = t_cols[...] + step * next_cols
            s_cols[...] = jnp.where(restart, total_cols / weight_total, next_cols)
            t_cols[...] = jnp.where(restart, 0.0, total_cols)
            scalars[0:1, :] = new_step
            scalars[1:2, :] = jnp.where(restart, new_weight, weight)
            scalars[2:3, :] = jnp.where(restart, 0.0, weight_total)

        return 0

    lax.fori_loop(0, STEPS, iteration, 0)


def per_device(
    tiles, tile_rows, tile_cols, tile_counts, objective, upper, bound_codes, rhs, row_codes
):
    blocked = lambda v: v.reshape(GRID, TILE)
    block = lambda dtype: pltpu.VMEM((GRID, TILE), dtype)
    anywhere = pl.BlockSpec(memory_space=pl.ANY)
    vmem = pl.BlockSpec(memory_space=pltpu.VMEM)
    dma = pltpu.SemaphoreType.DMA
    primal, dual = pl.pallas_call(
        kernel,
        out_shape=(jax.ShapeDtypeStruct((GRID, TILE), F32),) * 2,
        in_specs=[anywhere] * 9,
        out_specs=(vmem, vmem),
        scratch_shapes=[
            pltpu.VMEM((SLOTS, TILE, TILE), F32),
            pltpu.SMEM((SLOTS,), jnp.int32),
            pltpu.SMEM((SLOTS,), jnp.int32),
            pltpu.SMEM((1,), jnp.int32),
            block(F32), block(F32), block(jnp.int32), block(F32), block(jnp.int32),
            pltpu.VMEM((PAIRS, 2 * TILE, 2 * TILE), BF16),
            pltpu.VMEM((PAIRS, 2 * TILE, 2 * TILE), BF16),
            pltpu.VMEM((FULL, 2 * TILE), BF16),
            pltpu.VMEM((FULL + SLOTS, TILE), BF16),
        ]
        + [pltpu.VMEM((FULL, TILE), F32) for _ in range(15)]
        + [
            pltpu.VMEM((8, TILE), F32),
            pltpu.VMEM((2, GROUP, ROOM, TILE), F32),
            pltpu.VMEM((2, CHIPS, ROOM, TILE), F32),
            pltpu.VMEM((FULL + 8, TILE), F32),
            pltpu.VMEM((2, FULL + 8, TILE), F32),
            pltpu.VMEM((GROUP, 8, TILE), F32),
            pltpu.VMEM((GROUP, 8, TILE), F32),
            pltpu.VMEM((SLOTS, TILE), F32),
            pltpu.VMEM((SLOTS, TILE), F32),
            dma((9,)), dma, dma((2,)), dma, dma((2,)), dma, dma((2,)), dma((6,)),
        ],
        compiler_params=pltpu.CompilerParams(collective_id=0, has_side_effects=True),
        name="pdlp",
    )(
        tiles.reshape(SLOTS, TILE, TILE),
        tile_rows.reshape(SLOTS),
        tile_cols.reshape(SLOTS),
        tile_counts.reshape(1),
        blocked(objective),
        blocked(upper),
        blocked(bound_codes),
        blocked(rhs),
        blocked(row_codes),
    )
    return primal.reshape(-1), dual.reshape(-1)


def solution(mesh):
    placed = (
        P("row", "col", None, None, None),
        P("row", "col", None),
        P("row", "col", None),
        P("row", "col"),
        P("col"),
        P("col"),
        P("col"),
        P("row"),
        P("row"),
    )
    return jax.shard_map(
        per_device, mesh=mesh, in_specs=placed, out_specs=(P("col"), P("row")), check_vma=False
    )
```

time: 113 us -> 111 us (0.982)
  Pallas kernels: 110 us -> 107 us
    pallas_call x1, Pallas kernels: 110 us -> 107 us  [per_device(): pl.pallas_call(kernel, out_shape=(jax.ShapeDtypeStruct((GRID, TILE), F32)...]
where the time goes in v2:
time: 111 us
  Pallas kernels  107 us (96%)
  local copies, waits for them, and re-layouts  2 us (2%)
  between operations  1.29 us (1%)
    pallas_call x1, Pallas kernels, per_device(): pl.pallas_call(kernel, out_shape=(jax.ShapeDtypeStruct((GRID, TILE), F32)...  107 us

profile of v2, /device:TPU:1, one launch (start us, length us, event | category | flops | bytes accessed | tf_op | source)
XLA Modules:
  0.0 110.8 jit_solution(1047147602256693881)
XLA Ops:
  1.3 107.5 %pdlp.1 = (f32[64,128]{1,0:T(8,128)}, f32[64,128]{1,0:T(8,128)}) custom-call(f32[16,128,128]{2,1,0:T(8,128)} %bitcast.12, s32[16]{0:T(128)} %bitcast.20, s32[16]{0:T(128)} %bitcast.21, s32[1]{0:T(128)} %bitcast.11.counts_hbm, f32[64,128]{1,0:T(8,128)} %bitcast.13, f32[64,128]{1,0:T(8,128)} %bitcast.14, s32[64,128]{1,0:T(8,128)} %bitcast.15, ...), custom_call_target="tpu_custom_call" | custom-call | tf_op jit(solution)/shard_map/pdlp/pallas_call | solution.py:332
  108.8 0.0 copy-start
  108.8 1.4 %copy.14 = f32[8192]{0:T(1024)} copy(f32[8192]{0:T(1024)} %bitcast.19) | data formatting | bytes 65536
  110.1 0.0 copy-done
  110.1 0.6 copy.15
Async XLA Ops:
  108.8 1.4 %copy-start = (f32[64,128]{1,0:T(8,128)S(1)}, f32[64,128]{1,0:T(8,128)}, u32[]{:S(2)}) copy-start(f32[64,128]{1,0:T(8,128)} %get-tuple-element.5) | copy-start | bytes 98308
